TPU v7x, 32 devices: a whole 2x2x4 slice. The times are simulated.
32 devices in a mesh: groups: 2 (over y), seq: 16 (over z, x, core).
Axes of the slice: x: 2, y: 2, z: 4, core: 2. Of those that a mesh axis runs over, the one named last changes fastest.
Arguments:
- tokens: bfloat16 [4096, 256], P(('groups', 'seq')), parts along dimension 0, may hold values from -6 to 6
- inv_rms_a: float32 [4096], P(('groups', 'seq')), parts along dimension 0, may hold values from 0.5 to 2
- gain_a: float32 [256], replicated, may hold values from 0.1 to 1.9
- proj_a: bfloat16 [256, 768], replicated, may hold values from -0.375 to 0.375
- taps_a: bfloat16 [128, 256], replicated, may hold values from -0.5 to 0.5
- out_a: bfloat16 [256, 256], replicated, may hold values from -0.375 to 0.375
- inv_rms_b: float32 [4096], P(('groups', 'seq')), parts along dimension 0, may hold values from 0.5 to 2
- gain_b: float32 [256], replicated, may hold values from 0.1 to 1.9
- proj_b: bfloat16 [256, 768], replicated, may hold values from -0.375 to 0.375
- rates_b: float32 [16, 256], replicated, may hold values from 1.4648438e-06 to 0.033
- residues_b: float32 [16, 256], replicated, may hold values from -4 to 4
- out_b: bfloat16 [256, 256], replicated, may hold values from -0.375 to 0.375
Outputs:
- partial_a: bfloat16 [4096, 256], P(('groups', 'seq')), parts along dimension 0
- partial_b: bfloat16 [4096, 256], P(('groups', 'seq')), parts along dimension 0
There are 2 independent parts, one for each index of `groups`. A program takes and returns all parts, laid end to end along the dimension named above; an argument that names none is the same for every part. Nothing has to cross between parts.
All inputs are finite; a program needn't handle non-finite values.
Results may differ from a plain program's by a relative error of at most 0.019.
Values may be sent and summed in bfloat16 or wider, within the bound.
A program may use at most 64 MiB of HBM per device.

v0:
```python
import math

import jax
import jax.numpy as jnp
from jax import lax
from jax.sharding import PartitionSpec as P

HIGHEST_PREC = lax.Precision.HIGHEST


def from_behind(block, axis, distance):
    devices = range(lax.axis_size(axis))
    route = [(i - distance, i) for i in devices if i - distance in devices]
    return lax.ppermute(block, axis, route)


def rms_scale(values, inv_rms, gain):
    floats = values.astype(jnp.float32)
    return (floats * inv_rms[:, None] * gain).astype(jnp.bfloat16)


def mode_weights(rates, residues, length):
    energy = -jnp.expm1(-2.0 * rates) / -jnp.expm1(-2.0 * rates * length)
    return residues * jnp.sqrt(energy)


def matmul(form, left, right):
    return jnp.einsum(form, left, right, precision=HIGHEST_PREC)


def short_conv(product, rim_part, taps):
    tok_rows, feat_width = product.shape
    extended = jnp.concatenate([rim_part, product], 0)[None]
    kernel = jnp.flip(taps, 0)[:, None, :]
    result = lax.conv_general_dilated(
        extended,
        kernel,
        (1,),
        [(0, 0)],
        dimension_numbers=("NHC", "HIO", "NHC"),
        feature_group_count=feat_width,
        preferred_element_type=jnp.float32,
    )
    return result[0, 1:]


def dft_table(row_count, col_count, modulus):
    row_ids = lax.broadcasted_iota(jnp.int32, (row_count, col_count), 0)
    col_ids = lax.broadcasted_iota(jnp.int32, (row_count, col_count), 1)
    angles = (row_ids * col_ids % modulus).astype(jnp.float32) * (2.0 * math.pi / modulus)
    return (jnp.cos(angles), jnp.sin(angles))


def forward_transform(values, tables):
    cos_outer, sin_outer, cos_twist, sin_twist, cos_inner, sin_inner = tables
    segment_re = matmul("kn,cnq->ckq", cos_outer, values)
    segment_im = -matmul("kn,cnq->ckq", sin_outer, values)
    twist_re = segment_re * cos_twist + segment_im * sin_twist
    twist_im = segment_im * cos_twist - segment_re * sin_twist
    spec_re = matmul("ckn,nm->ckm", twist_re, cos_inner) + matmul(
        "ckn,nm->ckm", twist_im, sin_inner
    )
    spec_im = matmul("ckn,nm->ckm", twist_im, cos_inner) - matmul(
        "ckn,nm->ckm", twist_re, sin_inner
    )
    return (spec_re, spec_im)


def inverse_transform(spec_re, spec_im, tables, fft_len):
    cos_outer, sin_outer, cos_twist, sin_twist, cos_inner, sin_inner = tables
    back_re = matmul("ckn,nm->ckm", spec_re, cos_inner) - matmul("ckn,nm->ckm", spec_im, sin_inner)
    back_im = matmul("ckn,nm->ckm", spec_im, cos_inner) + matmul("ckn,nm->ckm", spec_re, sin_inner)
    turned_re = back_re * cos_twist - back_im * sin_twist
    turned_im = back_im * cos_twist + back_re * sin_twist
    half_rows = cos_outer.shape[1]
    real_part = matmul("kn,ckq->cnq", cos_outer, turned_re) - matmul(
        "kn,ckq->cnq", sin_outer, turned_im
    )
    return real_part / float(fft_len)


def sampled_filter(rates, weights, devices, tok_rows):
    dev_ids = lax.broadcasted_iota(jnp.int32, (devices, tok_rows), 0)
    row_ids = lax.broadcasted_iota(jnp.int32, (devices, tok_rows), 1)
    positions = (dev_ids * tok_rows + row_ids).astype(jnp.float32)
    terms = weights[:, :, None, None] * jnp.exp(-rates[:, :, None, None] * positions[None, None])
    return jnp.sum(terms, axis=0)


def spectral_conv(received, rates, residues, devices, tok_rows):
    chan_count = received.shape[0]
    fft_len = 2 * devices * tok_rows
    cos_outer, sin_outer = dft_table(2 * devices, devices, 2 * devices)
    cos_twist, sin_twist = dft_table(2 * devices, tok_rows, fft_len)
    cos_inner, sin_inner = dft_table(tok_rows, tok_rows, tok_rows)
    tables = (cos_outer, sin_outer, cos_twist, sin_twist, cos_inner, sin_inner)
    weights = mode_weights(rates, residues, float(devices * tok_rows))
    data_re, data_im = forward_transform(
        received.astype(jnp.float32).reshape(chan_count, devices, tok_rows), tables
    )
    filt_re, filt_im = forward_transform(sampled_filter(rates, weights, devices, tok_rows), tables)
    prod_re = data_re * filt_re - data_im * filt_im
    prod_im = data_re * filt_im + data_im * filt_re
    return inverse_transform(prod_re, prod_im, tables, fft_len).reshape(
        chan_count, devices * tok_rows
    )


def on_device(
    tokens,
    inv_rms_a,
    gain_a,
    proj_a,
    taps_a,
    out_a,
    inv_rms_b,
    gain_b,
    proj_b,
    rates_b,
    residues_b,
    out_b,
):
    tok_rows, feat_width = tokens.shape
    tap_count = taps_a.shape[0]
    normed = rms_scale(tokens, inv_rms_a, gain_a)
    projected = jnp.dot(normed, proj_a, preferred_element_type=jnp.float32)
    queries = projected[:, :feat_width]
    product = (projected[:, feat_width : 2 * feat_width] * projected[:, 2 * feat_width :]).astype(
        jnp.bfloat16
    )
    rim_part = from_behind(product, "seq", 1)
    short_out = short_conv(product, rim_part, taps_a)
    gated_a = (queries * short_out).astype(jnp.bfloat16)
    partial_a = jnp.dot(gated_a, out_a, preferred_element_type=jnp.float32).astype(jnp.bfloat16)
    hidden = (tokens.astype(jnp.float32) + partial_a.astype(jnp.float32)).astype(jnp.bfloat16)
    normed_b = rms_scale(hidden, inv_rms_b, gain_b)
    projected_b = lax.dot_general(
        proj_b, normed_b, (((0,), (1,)), ((), ())), preferred_element_type=jnp.float32
    )
    queries_b = projected_b[:feat_width]
    signal = (projected_b[feat_width : 2 * feat_width] * projected_b[2 * feat_width :]).astype(
        jnp.bfloat16
    )
    devices = lax.axis_size("seq")
    chan_count = feat_width // devices
    received = lax.all_to_all(signal, "seq", split_axis=0, concat_axis=1, tiled=True)
    offset = lax.axis_index("seq") * chan_count
    local_rates = lax.dynamic_slice_in_dim(rates_b, offset, chan_count, 1)
    residues = lax.dynamic_slice_in_dim(residues_b, offset, chan_count, 1)
    filtered = spectral_conv(received, local_rates, residues, devices, tok_rows).astype(
        jnp.bfloat16
    )
    long_out = lax.all_to_all(filtered, "seq", split_axis=1, concat_axis=0, tiled=True)
    long_out = lax.optimization_barrier(long_out)
    gated_b = (queries_b * long_out.astype(jnp.float32)).astype(jnp.bfloat16)
    partial_b = lax.dot_general(
        gated_b, out_b, (((0,), (0,)), ((), ())), preferred_element_type=jnp.float32
    ).astype(jnp.bfloat16)
    return (partial_a, partial_b)


def solution(mesh):
    placed = (
        P(("groups", "seq"), None),
        P(("groups", "seq")),
        P(),
        P(),
        P(),
        P(),
        P(("groups", "seq")),
        P(),
        P(),
        P(),
        P(),
        P(),
    )
    return jax.shard_map(
        on_device,
        mesh=mesh,
        in_specs=placed,
        out_specs=(P(("groups", "seq"), None), P(("groups", "seq"), None)),
        check_vma=False,
    )
```

profile of v0, /device:TPU:0, one launch (start us, length us, event | category | flops | bytes accessed | tf_op | source)
XLA Modules:
  0.0 44.7 jit_solution(11224540105381886314)
XLA Ops:
  0.7 1.0 %copy-done = bf16[256,768]{1,0:T(8,128)(2,1)S(1)} copy-done((bf16[256,768]{1,0:T(8,128)(2,1)S(1)}, bf16[256,768]{1,0:T(8,128)(2,1)}, u32[]{:S(2)}) %copy-start) | copy-done | bytes 393240
  1.6 1.1 %fusion.36 = f32[128,768]{1,0:T(8,128)S(1)} fusion(bf16[256,768]{1,0:T(8,128)(2,1)S(1)} %copy-done, bf16[128,256]{1,0:T(8,128)(2,1)} %param.12, f32[256]{0:T(256)} %param.14, f32[128]{0:T(128)} %param.13), kind=kOutput, calls=%fused_computation.65 | convolution fusion | flops 50462720 | bytes 853504 | tf_op jit(solution)/shard_map/dot_general | solution.py:126
  2.8 2.4 %collective-permute-start = (bf16[128,256]{1,0:T(8,128)(2,1)S(1)}, bf16[128,256]{1,0:T(8,128)(2,1)S(1)}, u32[]{:S(2)}, u32[]{:S(2)}) collective-permute-start(bf16[128,256]{1,0:T(8,128)(2,1)S(1)} %fusion.19), channel_id=1, source_target_pairs={{0,1},{1,2},{2,3},{3,4},{4,5},{5,6},{6,7},{7,8},{8,9},{9,10},{10,1... | collective-permute-start | bytes 196616 | tf_op jit(solution)/shard_map/ppermute | solution.py:14
  5.5 0.7 %multiply_reduce_fusion = f32[16,16,128]{2,1,0:T(8,128)S(1)} fusion(f32[16,128]{1,0:T(8,128)S(1)} %add_convert_fusion, f32[16,16]{1,0:T(8,128)S(1)} %get-tuple-element.5, f32[16,16]{1,0:T(8,128)S(1)} %get-tuple-element.4), kind=kLoop, calls=%fused_computation | loop fusion | flops 1540096 | bytes 141312 | tf_op jit(solution)/shard_map/reduce_sum | solution.py:87
  6.2 0.5 %fusion = f32[16,32,128]{2,1,0:T(8,128)S(1)} fusion(f32[16,16,128]{2,1,0:T(8,128)S(1)} %multiply_reduce_fusion), kind=kOutput, calls=%fused_computation.9 | convolution fusion | flops 12655616 | bytes 393216 | tf_op jit(solution)/shard_map/kn,cnq->ckq/dot_general | solution.py:28
  7.1 0.6 %fusion.29 = f32[16,32,128]{2,1,0:T(8,128)S(1)} fusion(f32[16,32,128]{2,1,0:T(8,128)S(1)} %convolution_bitcast_fusion.1, f32[16,32,128]{2,1,0:T(8,128)S(1)} %fusion, f32[32,128]{1,0:T(8,128)S(1)} %get-tuple-element.6, f32[32,128]{1,0:T(8,128)S(1)} %get-tuple-element.7), kind=kOutput, calls=%fused_computation.61 | convolution fusion | flops 101089280 | bytes 819200 | tf_op jit(solution)/shard_map/ckn,nm->ckm/dot_general | solution.py:28
  7.7 0.6 %convolution_subtract_fusion.1 = f32[16,32,128]{2,1,0:T(8,128)S(1)} fusion(f32[16,32,128]{2,1,0:T(8,128)S(1)} %fusion.29, f32[16,32,128]{2,1,0:T(8,128)S(1)} %fusion, f32[16,32,128]{2,1,0:T(8,128)S(1)} %convolution_bitcast_fusion.1, f32[32,128]{1,0:T(8,128)S(1)} %get-tuple-element.6, f32[32,128]{1,0:T(8,128)S(1)} %get-tuple-element.7), kind=kOutput, calls=%fused_computation.4 | convolution fusion | flops 101154816 | bytes 1081344 | tf_op jit(solution)/shard_map/ckn,nm->ckm/dot_general | solution.py:28
  8.4 0.6 %fusion.28 = f32[16,32,128]{2,1,0:T(8,128)S(1)} fusion(f32[16,32,128]{2,1,0:T(8,128)S(1)} %fusion, f32[16,32,128]{2,1,0:T(8,128)S(1)} %convolution_bitcast_fusion.1, f32[32,128]{1,0:T(8,128)S(1)} %get-tuple-element.6, f32[32,128]{1,0:T(8,128)S(1)} %get-tuple-element.7), kind=kOutput, calls=%fused_computation.60 | convolution fusion | flops 101089280 | bytes 819200 | tf_op jit(solution)/shard_map/ckn,nm->ckm/dot_general | solution.py:28
  9.3 2.0 %fusion.5 = f32[1,128,256]{2,0,1:T(1,128)S(1)} fusion(bf16[1,256,256]{2,1,0:T(8,128)(2,1)S(1)} %maximum_bitcast_fusion, bf16[128,1,256]{2,0,1:T(8,128)(2,1)S(1)} %bitcast.80), kind=kOutput, calls=%fused_computation.20 | convolution fusion | flops 8388608 | bytes 327680 | tf_op jit(solution)/shard_map/slice | solution.py:44
  11.5 0.8 %copy-done.1 = bf16[256,768]{1,0:T(8,128)(2,1)S(1)} copy-done((bf16[256,768]{1,0:T(8,128)(2,1)S(1)}, bf16[256,768]{1,0:T(8,128)(2,1)}, u32[]{:S(2)}) %copy-start.1) | copy-done | bytes 393240
  13.0 0.7 %copy.32 = bf16[256,128]{1,0:T(8,128)(2,1)} copy(bf16[256,128]{0,1:T(8,128)(2,1)S(1)} %fusion.17) | data formatting | bytes 131072 | tf_op jit(solution)/shard_map/convert_element_type | solution.py:141
  13.7 7.2 %all-to-all-start = ((bf16[16,16,128]{2,1,0:T(8,128)(2,1)}), bf16[16,16,128]{2,1,0:T(8,128)(2,1)S(1)}, u32[]{:S(2)}, u32[]{:S(2)}) async-start(bf16[16,16,128]{2,1,0:T(8,128)(2,1)} %bitcast.3), calls=%async_computation | async-start | bytes 131072 | tf_op jit(solution)/shard_map/all_to_all | solution.py:146
  20.9 0.6 %convolution_add_fusion.1 = f32[16,32,128]{2,1,0:T(8,128)S(1)} fusion(f32[16,32,128]{2,1,0:T(8,128)S(1)} %fusion.28, f32[16,32,128]{2,1,0:T(8,128)S(1)} %convolution_bitcast_fusion.1, f32[16,32,128]{2,1,0:T(8,128)S(1)} %fusion, f32[32,128]{1,0:T(8,128)S(1)} %get-tuple-element.6, f32[32,128]{1,0:T(8,128)S(1)} %get-tuple-element.7), kind=kOutput, calls=%fused_computation.6 | convolution fusion | flops 101154816 | bytes 1081344 | tf_op jit(solution)/shard_map/ckn,nm->ckm/dot_general | solution.py:28
  21.5 6.3 %all-to-all-done = bf16[16,16,128]{2,1,0:T(8,128)(2,1)S(1)} async-done(((bf16[16,16,128]{2,1,0:T(8,128)(2,1)}), bf16[16,16,128]{2,1,0:T(8,128)(2,1)S(1)}, u32[]{:S(2)}, u32[]{:S(2)}) %all-to-all-start) | async-done | bytes 65568 | tf_op jit(solution)/shard_map/all_to_all | solution.py:146
  28.5 0.6 %fusion.27 = f32[16,32,128]{2,1,0:T(8,128)S(1)} fusion(f32[16,32,128]{2,1,0:T(8,128)S(1)} %convolution_bitcast_fusion.2, f32[16,32,128]{2,1,0:T(8,128)S(1)} %fusion.1, f32[32,128]{1,0:T(8,128)S(1)} %get-tuple-element.6, f32[32,128]{1,0:T(8,128)S(1)} %get-tuple-element.7), kind=kOutput, calls=%fused_computation.59 | convolution fusion | flops 101089280 | bytes 819200 | tf_op jit(solution)/shard_map/ckn,nm->ckm/dot_general | solution.py:28
  29.2 0.6 %fusion.26 = f32[16,32,128]{2,1,0:T(8,128)S(1)} fusion(f32[16,32,128]{2,1,0:T(8,128)S(1)} %fusion.1, f32[16,32,128]{2,1,0:T(8,128)S(1)} %convolution_bitcast_fusion.2, f32[32,128]{1,0:T(8,128)S(1)} %get-tuple-element.6, f32[32,128]{1,0:T(8,128)S(1)} %get-tuple-element.7), kind=kOutput, calls=%fused_computation.58 | convolution fusion | flops 101089280 | bytes 819200 | tf_op jit(solution)/shard_map/ckn,nm->ckm/dot_general | solution.py:28
  29.8 0.6 %convolution_add_fusion.2 = f32[16,32,128]{2,1,0:T(8,128)S(1)} fusion(f32[16,32,128]{2,1,0:T(8,128)S(1)} %fusion.26, f32[16,32,128]{2,1,0:T(8,128)S(1)} %convolution_bitcast_fusion.2, f32[16,32,128]{2,1,0:T(8,128)S(1)} %fusion.1, f32[32,128]{1,0:T(8,128)S(1)} %get-tuple-element.6, f32[32,128]{1,0:T(8,128)S(1)} %get-tuple-element.7), kind=kOutput, calls=%fused_computation.7 | convolution fusion | flops 101154816 | bytes 1081344 | tf_op jit(solution)/shard_map/ckn,nm->ckm/dot_general | solution.py:28
  30.4 0.6 %multiply_subtract_fusion = (f32[16,32,128]{2,1,0:T(8,128)S(1)}, f32[16,32,128]{2,1,0:T(8,128)S(1)}) fusion(f32[16,32,128]{2,1,0:T(8,128)S(1)} %convolution_subtract_fusion.1, f32[16,32,128]{2,1,0:T(8,128)S(1)} %convolution_add_fusion.2, f32[16,32,128]{2,1,0:T(8,128)S(1)} %convolution_add_fusion.1, f32[16,32,128]{2,1,0:T(8,128)S(1)} %fusion.27, ...), kind=kOutput, calls=%fused_computation.30 | convolution fusion | flops 101548032 | bytes 2129920 | tf_op jit(solution)/shard_map/ckn,nm->ckm/dot_general | solution.py:28
  31.1 0.6 %fusion.46 = f32[16,32,128]{2,1,0:T(8,128)S(1)} fusion(f32[16,32,128]{2,1,0:T(8,128)S(1)} %get-tuple-element.2), kind=kOutput, calls=%fused_computation.74 | convolution fusion | flops 100892672 | bytes 524288 | tf_op jit(solution)/shard_map/ckn,nm->ckm/dot_general | solution.py:28
  31.7 0.6 %fusion.44 = f32[16,32,128]{2,1,0:T(8,128)S(1)} fusion(f32[16,32,128]{2,1,0:T(8,128)S(1)} %get-tuple-element.3), kind=kOutput, calls=%fused_computation.72 | convolution fusion | flops 100892672 | bytes 524288 | tf_op jit(solution)/shard_map/ckn,nm->ckm/dot_general | solution.py:28
  32.3 0.6 %convolution_subtract_fusion = f32[16,32,128]{2,1,0:T(8,128)S(1)} fusion(f32[16,32,128]{2,1,0:T(8,128)S(1)} %fusion.46, f32[16,32,128]{2,1,0:T(8,128)S(1)} %get-tuple-element.3), kind=kOutput, calls=%fused_computation.3 | convolution fusion | flops 100958208 | bytes 786432 | tf_op jit(solution)/shard_map/ckn,nm->ckm/dot_general | solution.py:28
  32.9 0.6 %convolution_add_fusion = f32[16,32,128]{2,1,0:T(8,128)S(1)} fusion(f32[16,32,128]{2,1,0:T(8,128)S(1)} %fusion.44, f32[16,32,128]{2,1,0:T(8,128)S(1)} %get-tuple-element.2), kind=kOutput, calls=%fused_computation.2 | convolution fusion | flops 100958208 | bytes 786432 | tf_op jit(solution)/shard_map/ckn,nm->ckm/dot_general | solution.py:28
  34.3 9.5 %all_to_all.32 = bf16[16,16,128]{2,0,1:T(8,128)(2,1)S(1)} all-to-all(bf16[16,16,128]{2,0,1:T(8,128)(2,1)S(1)} %copy.34), channel_id=1, replica_groups=mesh['groups'=2,'seq'=16] {'seq'}, dimensions={1} | all-to-all | bytes 131072 | tf_op jit(solution)/shard_map/all_to_all | solution.py:153
  43.9 0.8 %convolution_convert_fusion = bf16[128,256]{1,0:T(8,128)(2,1)} fusion(bf16[256,256]{1,0:T(8,128)(2,1)S(1)} %copy-done.5, f32[768,128]{0,1:T(8,128)S(1)} %convolution_bitcast_fusion, bf16[256,128]{0,1:T(8,128)(2,1)S(1)} %copy.35), kind=kOutput, calls=%fused_computation.17 | convolution fusion | flops 16908288 | bytes 393216 | tf_op jit(solution)/shard_map/dot_general | solution.py:156
  (38 shorter events, 3.4 us)
Async XLA Ops:
  0.6 1.0 %copy-start = (bf16[256,768]{1,0:T(8,128)(2,1)S(1)}, bf16[256,768]{1,0:T(8,128)(2,1)}, u32[]{:S(2)}) copy-start(bf16[256,768]{1,0:T(8,128)(2,1)} %param.15) | copy-start | bytes 1179652
  0.6 4.7 %copy-start.7 = (f32[16,256]{1,0:T(8,128)S(1)}, f32[16,256]{1,0:T(8,128)}, u32[]{:S(2)}) copy-start(f32[16,256]{1,0:T(8,128)} %param.22) | copy-start | bytes 49156
  0.7 4.7 %copy-start.8 = (f32[16,256]{1,0:T(8,128)S(1)}, f32[16,256]{1,0:T(8,128)}, u32[]{:S(2)}) copy-start(f32[16,256]{1,0:T(8,128)} %param.21) | copy-start | bytes 49156
  2.8 6.5 %collective-permute-start = (bf16[128,256]{1,0:T(8,128)(2,1)S(1)}, bf16[128,256]{1,0:T(8,128)(2,1)S(1)}, u32[]{:S(2)}, u32[]{:S(2)}) collective-permute-start(bf16[128,256]{1,0:T(8,128)(2,1)S(1)} %fusion.19), channel_id=1, source_target_pairs={{0,1},{1,2},{2,3},{3,4},{4,5},{5,6},{6,7},{7,8},{8,9},{9,10},{10,1... | collective-permute-start | bytes 196616 | tf_op jit(solution)/shard_map/ppermute | solution.py:14
  8.4 0.8 %copy-start.6 = (bf16[128,256]{1,0:T(8,128)(2,1)S(1)}, bf16[128,256]{1,0:T(8,128)(2,1)}, u32[]{:S(2)}) copy-start(bf16[128,256]{1,0:T(8,128)(2,1)} %param.16) | copy-start | bytes 196612
  9.3 2.0 %copy-start.4 = (bf16[256,256]{1,0:T(8,128)(2,1)S(1)}, bf16[256,256]{1,0:T(8,128)(2,1)}, u32[]{:S(2)}) copy-start(bf16[256,256]{1,0:T(8,128)(2,1)} %param.17) | copy-start | bytes 393220
  9.3 2.2 %copy-start.9 = (f32[256]{0:T(256)S(1)}, f32[256]{0:T(256)}, u32[]{:S(2)}) copy-start(f32[256]{0:T(256)} %param.19) | copy-start | bytes 3076
  9.3 2.2 %copy-start.10 = (f32[128]{0:T(128)S(1)}, f32[128]{0:T(128)}, u32[]{:S(2)}) copy-start(f32[128]{0:T(128)} %param.18) | copy-start | bytes 1540
  11.3 1.0 %copy-start.1 = (bf16[256,768]{1,0:T(8,128)(2,1)S(1)}, bf16[256,768]{1,0:T(8,128)(2,1)}, u32[]{:S(2)}) copy-start(bf16[256,768]{1,0:T(8,128)(2,1)} %param.20) | copy-start | bytes 1179652
  11.3 1.0 %copy-start.2 = (bf16[128,256]{1,0:T(8,128)(2,1)S(1)}, bf16[128,256]{1,0:T(8,128)(2,1)}, u32[]{:S(2)}) copy-start(bf16[128,256]{1,0:T(8,128)(2,1)} %param.12) | copy-start | bytes 196612
  12.3 0.6 %copy-start.3 = (bf16[128,256]{1,0:T(8,128)(2,1)}, bf16[128,256]{1,0:T(8,128)(2,1)S(1)}, u32[]{:S(2)}) copy-start(bf16[128,256]{1,0:T(8,128)(2,1)S(1)} %convolution_convert_fusion.1) | copy-start | bytes 196612
  13.7 14.1 %all-to-all-start = ((bf16[16,16,128]{2,1,0:T(8,128)(2,1)}), bf16[16,16,128]{2,1,0:T(8,128)(2,1)S(1)}, u32[]{:S(2)}, u32[]{:S(2)}) async-start(bf16[16,16,128]{2,1,0:T(8,128)(2,1)} %bitcast.3), calls=%async_computation | async-start | bytes 131072 | tf_op jit(solution)/shard_map/all_to_all | solution.py:146
  33.9 10.0 %copy-start.5 = (bf16[256,256]{1,0:T(8,128)(2,1)S(1)}, bf16[256,256]{1,0:T(8,128)(2,1)}, u32[]{:S(2)}) copy-start(bf16[256,256]{1,0:T(8,128)(2,1)} %param.23) | copy-start | bytes 393220
where the time goes:
time: 45.1 us; the launch traced here: 44.7 us
  matrix products  14 us (31%)
  starting transfers between devices  9.58 us (21%)
  blocking collectives  9.48 us (21%)
  waiting for transfers between devices  6.28 us (14%)
  local copies, waits for them, and re-layouts  3.35 us (7%)
  other arithmetic  1.02 us (2%)
  between operations  1.02 us (2%)
    dot_general x18, matrix products, matmul(): return jnp.einsum(form, left, right, precision=HIGHEST_PREC)  9.69 us
    all_to_all x1, blocking collectives, on_device(): lax.all_to_all(filtered, 'seq', split_axis=1, concat_axis=0, tiled=True)  9.48 us
    all_to_all x1, starting transfers between devices, on_device(): lax.all_to_all(signal, 'seq', split_axis=0, concat_axis=1, tiled=True)  7.18 us
    all_to_all x1, waiting for transfers between devices, on_device(): lax.all_to_all(signal, 'seq', split_axis=0, concat_axis=1, tiled=True)  6.28 us
    unnamed x22, local copies, waits for them, and re-layouts  2.41 us
    ppermute x1, starting transfers between devices, from_behind(): return lax.ppermute(block, axis, route)  2.4 us
    slice x1, matrix products, short_conv(): return result[0, 1:]  1.96 us
    dot_general x1, matrix products, on_device(): projected = jnp.dot(normed, proj_a, preferred_element_type=jnp.float32)  1.1 us
  transfers between devices with their start and end apart: 2, of which 1 were waited for; matrix products, arithmetic and copies ran while one was open for 10% of the time, Pallas kernels for 0%

commit v1 on v0

v1 whole, which is shorter than its diff:
```python
import functools

import jax
import jax.numpy as jnp
import numpy as np
from jax import lax
from jax.experimental import pallas as pl
from jax.experimental.pallas import tpu as pltpu
from jax.sharding import PartitionSpec as P

MESH = pl.DeviceIdType.MESH
F32 = jnp.float32
BF16 = jnp.bfloat16
SUB = 8
LANES = 128


def dft_tables(rows):
    freq = (np.arange(rows) + 0.5)[:, None]
    angle = freq * np.arange(rows)[None, :] * (np.pi / rows)
    cos, sin = np.cos(angle), np.sin(angle)
    sign = np.where(np.arange(rows) % 2 == 0, 1.0, -1.0)[:, None]
    own = np.concatenate([cos, sin], 0)
    behind = np.concatenate([sign * sin, -sign * cos], 0)
    back = own.T / rows
    return [jnp.asarray(t, F32).astype(BF16) for t in (own, behind, back)]


def dot(left, right):
    return jnp.dot(left, right, preferred_element_type=F32)


def split(value):
    high = value.astype(BF16)
    return high, (value - high.astype(F32)).astype(BF16)


def one_minus_exp(a):
    series = 1.0 - a / 9.0
    for k in (8.0, 7.0, 6.0, 5.0, 4.0, 3.0, 2.0):
        series = 1.0 - series * a / k
    return jnp.where(a < 0.5, a * series, 1.0 - jnp.exp(-a))


def column(row):
    rows = row.shape[1]
    eye = lax.broadcasted_iota(jnp.int32, (rows, rows), 0) == lax.broadcasted_iota(
        jnp.int32, (rows, rows), 1
    )
    return jnp.sum(jnp.where(eye, row, 0.0), axis=1, keepdims=True)


def scaled(tokens, scale, gain):
    return (tokens.astype(F32) * scale * gain).astype(BF16)


def spectral_product(data, filt):
    half = data.shape[0] // 2
    dc, ds, fc, fs = data[:half], data[half:], filt[:half], filt[half:]
    return jnp.concatenate([dc * fc - ds * fs, dc * fs + ds * fc], 0).astype(BF16)


def modes_over_rows(first, step, out_ref):
    rows, width = out_ref.shape
    for lane in range(0, width, LANES):
        cols = slice(lane, lane + LANES)
        term, ratio = first[:, :, cols], step[:, :, cols]
        for a in range(rows // SUB):
            out_ref[a * SUB : (a + 1) * SUB, cols] = jnp.sum(term, axis=0)
            if a + 1 < rows // SUB:
                term = term * ratio


def end_state(signal_ref, step, last):
    rows, width = signal_ref.shape
    parts = []
    for lane in range(0, width, LANES):
        cols = slice(lane, lane + LANES)
        ratio = step[:, :, cols]
        total = jnp.broadcast_to(signal_ref[0:SUB, cols][None], ratio.shape)
        for a in range(1, rows // SUB):
            total = total * ratio + signal_ref[a * SUB : (a + 1) * SUB, cols][None]
        parts.append(jnp.sum(total * last[:, :, cols], axis=1))
    return jnp.concatenate(parts, 1)


def kernel(n, *refs):
    hbm = refs[:15]
    pa_ref, pb_ref = refs[15:17]
    vm = refs[17:32]
    (rim_ref, rim_rms_ref, filt_ref, signal_ref, carry_ref, state_ref, states_ref) = refs[32:39]
    (load_sem, rim_send, rim_recv, st_send, st_recv, out_sem, oa_ref, ob_ref) = refs[39:]
    me = lax.axis_index("seq")
    rows, width = vm[0].shape
    modes = vm[9].shape[0]

    barrier = pltpu.get_barrier_semaphore()

    @pl.loop(1, n)
    def _(i):
        pl.semaphore_signal(
            barrier, inc=1, device_id={"seq": lax.rem(me + i, n)}, device_id_type=MESH
        )

    loads = [pltpu.make_async_copy(h, v, load_sem.at[i]) for i, (h, v) in enumerate(zip(hbm, vm))]
    order = (0, 1, 2, 3, 12, 4, 9, 10, 13, 14, 5, 6, 7, 8, 11)
    for i in order:
        loads[i].start()
    (tok, rms_a, gain_a, proj_a, taps, out_a) = vm[:6]
    (rms_b, gain_b, proj_b, rates_ref, resid_ref, out_b, own_f, rim_f, back_f) = vm[6:]

    pl.semaphore_wait(barrier, n - 1)

    def rim_copies():
        target = {"seq": lax.rem(me + 1, n)}
        return [
            pltpu.make_async_remote_copy(
                src_ref=src,
                dst_ref=dst,
                send_sem=rim_send.at[i],
                recv_sem=rim_recv.at[i],
                device_id=target,
                device_id_type=MESH,
            )
            for i, (src, dst) in enumerate(((hbm[0], rim_ref), (hbm[1], rim_rms_ref)))
        ]

    @pl.when(me < n - 1)
    def _():
        for copy in rim_copies():
            copy.start()

    for i in (0, 1, 2, 3):
        loads[i].wait()
    normed = scaled(tok[...], column(rms_a[...]), gain_a[...])
    projected = dot(normed, proj_a[...])
    queries = projected[:, :width]
    product = (projected[:, width : 2 * width] * projected[:, 2 * width :]).astype(BF16)
    loads[12].wait()
    loads[4].wait()
    spectrum = dot(own_f[...], product)
    taps_spec = dot(own_f[...], taps[...])

    loads[9].wait()
    loads[10].wait()
    rates = rates_ref[...]
    length = float(n * rows)
    weights = resid_ref[...] * jnp.sqrt(
        one_minus_exp(2.0 * rates) / one_minus_exp(2.0 * rates * length)
    )
    rates3 = jnp.broadcast_to(rates[:, None, :], (modes, SUB, width))
    within = lax.broadcasted_iota(jnp.int32, (modes, SUB, width), 1).astype(F32)
    step = jnp.exp(-rates3 * float(SUB))
    lag = jnp.exp(-rates3 * within)
    last = jnp.exp(-rates3 * (SUB - 1.0 - within))
    read = jnp.exp(-rates3 * (within + 1.0))
    block = jnp.exp(-rates * float(rows))
    modes_over_rows(weights[:, None, :] * lag, step, filt_ref)
    high, low = split(filt_ref[...])
    long_spec = dot(own_f[...], high) + dot(own_f[...], low)
    for i in (13, 14, 5, 6, 7, 8, 11):
        loads[i].wait()
    scale_b = column(rms_b[...])

    @pl.when(me > 0)
    def _():
        for copy in rim_copies():
            copy.wait_recv()
        rim_normed = scaled(rim_ref[...], column(rim_rms_ref[...]), gain_a[...])
        pair = dot(rim_normed, proj_a[:, width:])
        rim_product = (pair[:, :width] * pair[:, width:]).astype(BF16)
        carry_ref[...] = dot(rim_f[...], rim_product)

    @pl.when(me == 0)
    def _():
        carry_ref[...] = jnp.zeros_like(carry_ref)

    short_out = dot(back_f[...], spectral_product(spectrum + carry_ref[...], taps_spec))
    gated_a = (queries * short_out).astype(BF16)
    partial_a = dot(gated_a, out_a[...]).astype(BF16)
    oa_ref[...] = partial_a
    copy_a = pltpu.make_async_copy(oa_ref, pa_ref, out_sem.at[0])
    copy_a.start()
    hidden = (tok[...].astype(F32) + partial_a.astype(F32)).astype(BF16)
    normed_b = scaled(hidden, scale_b, gain_b[...])
    pair_b = dot(normed_b, proj_b[:, width:])
    signal = (pair_b[:, :width] * pair_b[:, width:]).astype(BF16)
    signal_ref[...] = signal.astype(F32)
    state_ref[...] = end_state(signal_ref, step, last).astype(BF16)

    def state_copy(source, target):
        return pltpu.make_async_remote_copy(
            src_ref=state_ref,
            dst_ref=states_ref.at[source],
            send_sem=st_send.at[target],
            recv_sem=st_recv.at[source],
            device_id={"seq": target},
            device_id_type=MESH,
        )

    @pl.loop(0, n - 1 - me)
    def _(i):
        state_copy(me, n - 1 - i).start()

    queries_b = dot(normed_b, proj_b[:, :width])
    local = dot(back_f[...], spectral_product(dot(own_f[...], signal), long_spec))

    def gather(source, total):
        state_copy(source, lax.rem(me + 1, n)).wait_recv()
        return total * block + states_ref[source].astype(F32)

    total = lax.fori_loop(0, me, gather, jnp.zeros((modes, width), F32))
    modes_over_rows((total * weights)[:, None, :] * read, step, filt_ref)
    long_out = (local + filt_ref[...]).astype(BF16)
    gated_b = (queries_b * long_out.astype(F32)).astype(BF16)
    ob_ref[...] = dot(gated_b, out_b[...]).astype(BF16)
    copy_b = pltpu.make_async_copy(ob_ref, pb_ref, out_sem.at[1])
    copy_b.start()

    @pl.when(me < n - 1)
    def _():
        for copy in rim_copies():
            copy.wait_send()

    @pl.loop(0, n - 1 - me)
    def _(i):
        state_copy(me, n - 1 - i).wait_send()

    copy_a.wait()
    copy_b.wait()


def solution(mesh):
    n = mesh.shape["seq"]

    def on_device(*args):
        rows, width = args[0].shape
        modes = args[9].shape[0]
        args = [a[None] if a.ndim == 1 else a for a in args] + dft_tables(rows)
        block = jax.ShapeDtypeStruct((rows, width), BF16)
        anywhere = pl.BlockSpec(memory_space=pl.ANY)
        return pl.pallas_call(
            functools.partial(kernel, n),
            out_shape=(block, block),
            in_specs=[anywhere] * len(args),
            out_specs=(anywhere, anywhere),
            scratch_shapes=[pltpu.VMEM(a.shape, a.dtype) for a in args]
            + [
                pltpu.VMEM((rows, width), BF16),
                pltpu.VMEM((1, rows), F32),
                pltpu.VMEM((rows, width), F32),
                pltpu.VMEM((rows, width), F32),
                pltpu.VMEM((2 * rows, width), F32),
                pltpu.VMEM((modes, width), BF16),
                pltpu.VMEM((n, modes, width), BF16),
                pltpu.SemaphoreType.DMA((len(args),)),
                pltpu.SemaphoreType.DMA((2,)),
                pltpu.SemaphoreType.DMA((2,)),
                pltpu.SemaphoreType.DMA((n,)),
                pltpu.SemaphoreType.DMA((n,)),
                pltpu.SemaphoreType.DMA((2,)),
                pltpu.VMEM((rows, width), BF16),
                pltpu.VMEM((rows, width), BF16),
            ],
            compiler_params=pltpu.CompilerParams(collective_id=0, has_side_effects=True),
        )(*args)

    shard = P(("groups", "seq"))
    wide = P(("groups", "seq"), None)
    placed = (wide, shard, P(), P(), P(), P(), shard, P(), P(), P(), P(), P())
    return jax.shard_map(
        on_device, mesh=mesh, in_specs=placed, out_specs=(wide, wide), check_vma=False
    )
```

time: 45.1 us -> 16.7 us (0.37)
  the two profiles are of different devices: /device:TPU:0 before, /device:TPU:12 now
where the time goes in v1:
time: 16.7 us; the launch traced here: 16.5 us
  Pallas kernels  13.8 us (83%)
  local copies, waits for them, and re-layouts  2.14 us (13%)
  between operations  0.65 us (4%)
    pallas_call x1, Pallas kernels, on_device(): pl.pallas_call(functools.partial(kernel, n), out_shape=(block, block), in...  13.8 us
    unnamed x4, local copies, waits for them, and re-layouts  2.14 us

profile of v1, /device:TPU:12, one launch (start us, length us, event | category | flops | bytes accessed | tf_op | source)
XLA Modules:
  0.0 16.5 jit_solution(2439248622034736729)
XLA Ops:
  0.6 13.8 %shard_map.158 = (bf16[128,256]{1,0:T(8,128)(2,1)}, bf16[128,256]{1,0:T(8,128)(2,1)}) custom-call(bf16[128,256]{1,0:T(8,128)(2,1)} %refs_0_.1, f32[1,128]{1,0:T(1,128)} %bitcast.6, f32[1,256]{1,0:T(1,128)} %bitcast.4, bf16[256,768]{1,0:T(8,128)(2,1)} %refs_3_.1, bf16[128,256]{1,0:T(8,128)(2,1)} %refs_4_.1, bf16[256,256]{1,0:T(8,128)(2,1)} %refs_5_.1, ...), custom_call_target="tpu_custom_call" | custom-call | tf_op jit(solution)/shard_map/pallas_call | solution.py:242
  14.4 0.0 copy-start
  14.4 1.5 %copy.19 = bf16[128,256]{1,0:T(8,128)(2,1)} copy(bf16[128,256]{1,0:T(8,128)(2,1)} %get-tuple-element.4) | data formatting | bytes 131072
  15.9 0.0 copy-done
  15.9 0.6 %copy.20 = bf16[128,256]{1,0:T(8,128)(2,1)} copy(bf16[128,256]{1,0:T(8,128)(2,1)S(1)} %copy-done) | data formatting | bytes 131072
Async XLA Ops:
  14.4 1.5 %copy-start = (bf16[128,256]{1,0:T(8,128)(2,1)S(1)}, bf16[128,256]{1,0:T(8,128)(2,1)}, u32[]{:S(2)}) copy-start(bf16[128,256]{1,0:T(8,128)(2,1)} %get-tuple-element.5) | copy-start | bytes 196612

commit v2 on v1

--- a/solution.py
+++ b/solution.py
@@ -84,23 +84,53 @@
     return jnp.concatenate(parts, 1)
 
 
+def plane_size(n):
+    size = 1
+    while n % (2 * size) == 0 and 4 * size * size <= n:
+        size *= 2
+    return size
+
+
+def hand_out(a_ref, b_ref, pa_ref, pb_ref, sem):
+    copies = [
+        pltpu.make_async_copy(a_ref, pa_ref, sem.at[0]),
+        pltpu.make_async_copy(b_ref, pb_ref, sem.at[1]),
+    ]
+    for copy in copies:
+        copy.start()
+    for copy in copies:
+        copy.wait()
+
+
 def kernel(n, *refs):
     hbm = refs[:15]
     pa_ref, pb_ref = refs[15:17]
     vm = refs[17:32]
     (rim_ref, rim_rms_ref, filt_ref, signal_ref, carry_ref, state_ref, states_ref) = refs[32:39]
-    (load_sem, rim_send, rim_recv, st_send, st_recv, out_sem, oa_ref, ob_ref) = refs[39:]
+    (load_sem, rim_send, rim_recv, st_send, st_recv, far_sem) = refs[39:]
     me = lax.axis_index("seq")
     rows, width = vm[0].shape
     modes = vm[9].shape[0]
 
+    plane = plane_size(n)
+    planes = n // plane
+    level, place = me // plane, lax.rem(me, plane)
     barrier = pltpu.get_barrier_semaphore()
 
-    @pl.loop(1, n)
-    def _(i):
-        pl.semaphore_signal(
-            barrier, inc=1, device_id={"seq": lax.rem(me + i, n)}, device_id_type=MESH
-        )
+    def signal(sem, target):
+        pl.semaphore_signal(sem, inc=1, device_id={"seq": target}, device_id_type=MESH)
+
+    @pl.loop(1, plane)
+    def _(i):
+        signal(barrier, level * plane + lax.rem(place + i, plane))
+
+    @pl.loop(level + 1, planes)
+    def _(i):
+        signal(barrier, i * plane + place)
+
+    @pl.when(jnp.logical_and(place == 0, level > 0))
+    def _():
+        signal(barrier, me - 1)
 
     loads = [pltpu.make_async_copy(h, v, load_sem.at[i]) for i, (h, v) in enumerate(zip(hbm, vm))]
     order = (0, 1, 2, 3, 12, 4, 9, 10, 13, 14, 5, 6, 7, 8, 11)
@@ -109,7 +139,8 @@
     (tok, rms_a, gain_a, proj_a, taps, out_a) = vm[:6]
     (rms_b, gain_b, proj_b, rates_ref, resid_ref, out_b, own_f, rim_f, back_f) = vm[6:]
 
-    pl.semaphore_wait(barrier, n - 1)
+    crossing = jnp.logical_and(place == plane - 1, level < planes - 1)
+    pl.semaphore_wait(barrier, plane - 1 + level + crossing.astype(jnp.int32))
 
     def rim_copies():
         target = {"seq": lax.rem(me + 1, n)}
@@ -129,6 +160,10 @@
     def _():
         for copy in rim_copies():
             copy.start()
+
+    @pl.loop(0, level)
+    def _(i):
+        signal(far_sem, i * plane + place)
 
     for i in (0, 1, 2, 3):
         loads[i].wait()
@@ -178,9 +213,7 @@
     short_out = dot(back_f[...], spectral_product(spectrum + carry_ref[...], taps_spec))
     gated_a = (queries * short_out).astype(BF16)
     partial_a = dot(gated_a, out_a[...]).astype(BF16)
-    oa_ref[...] = partial_a
-    copy_a = pltpu.make_async_copy(oa_ref, pa_ref, out_sem.at[0])
-    copy_a.start()
+    pa_ref[...] = partial_a
     hidden = (tok[...].astype(F32) + partial_a.astype(F32)).astype(BF16)
     normed_b = scaled(hidden, scale_b, gain_b[...])
     pair_b = dot(normed_b, proj_b[:, width:])
@@ -198,6 +231,10 @@
             device_id_type=MESH,
         )
 
+    @pl.when(level < planes - 1)
+    def _():
+        pl.semaphore_wait(far_sem, planes - 1 - level)
+
     @pl.loop(0, n - 1 - me)
     def _(i):
         state_copy(me, n - 1 - i).start()
@@ -213,9 +250,7 @@
     modes_over_rows((total * weights)[:, None, :] * read, step, filt_ref)
     long_out = (local + filt_ref[...]).astype(BF16)
     gated_b = (queries_b * long_out.astype(F32)).astype(BF16)
-    ob_ref[...] = dot(gated_b, out_b[...]).astype(BF16)
-    copy_b = pltpu.make_async_copy(ob_ref, pb_ref, out_sem.at[1])
-    copy_b.start()
+    pb_ref[...] = dot(gated_b, out_b[...]).astype(BF16)
 
     @pl.when(me < n - 1)
     def _():
@@ -225,9 +260,6 @@
     @pl.loop(0, n - 1 - me)
     def _(i):
         state_copy(me, n - 1 - i).wait_send()
-
-    copy_a.wait()
-    copy_b.wait()
 
 
 def solution(mesh):
@@ -238,12 +270,14 @@
         modes = args[9].shape[0]
         args = [a[None] if a.ndim == 1 else a for a in args] + dft_tables(rows)
         block = jax.ShapeDtypeStruct((rows, width), BF16)
+        fast = pltpu.VMEM((rows, width), BF16)
+        inside = pl.BlockSpec(memory_space=pltpu.VMEM)
         anywhere = pl.BlockSpec(memory_space=pl.ANY)
-        return pl.pallas_call(
+        results = pl.pallas_call(
             functools.partial(kernel, n),
-            out_shape=(block, block),
+            out_shape=(fast, fast),
             in_specs=[anywhere] * len(args),
-            out_specs=(anywhere, anywhere),
+            out_specs=(inside, inside),
             scratch_shapes=[pltpu.VMEM(a.shape, a.dtype) for a in args]
             + [
                 pltpu.VMEM((rows, width), BF16),
@@ -258,12 +292,17 @@
                 pltpu.SemaphoreType.DMA((2,)),
                 pltpu.SemaphoreType.DMA((n,)),
                 pltpu.SemaphoreType.DMA((n,)),
-                pltpu.SemaphoreType.DMA((2,)),
-                pltpu.VMEM((rows, width), BF16),
-                pltpu.VMEM((rows, width), BF16),
+                pltpu.SemaphoreType.REGULAR,
             ],
             compiler_params=pltpu.CompilerParams(collective_id=0, has_side_effects=True),
         )(*args)
+        return pl.pallas_call(
+            hand_out,
+            out_shape=(block, block),
+            in_specs=[inside] * 2,
+            out_specs=(anywhere, anywhere),
+            scratch_shapes=[pltpu.SemaphoreType.DMA((2,))],
+        )(*[pltpu.with_memory_space_constraint(r, pltpu.VMEM) for r in results])
 
     shard = P(("groups", "seq"))
     wide = P(("groups", "seq"), None)

time: 16.7 us -> 11.8 us (0.71)
  the two profiles are of different devices: /device:TPU:12 before, /device:TPU:20 now
where the time goes in v2:
time: 11.8 us; the launch traced here: 11.7 us
  Pallas kernels  11 us (93%)
  between operations  0.64 us (5%)
    pallas_call x1, Pallas kernels, on_device(): pl.pallas_call(functools.partial(kernel, n), out_shape=(fast, fast), in_s...  10.4 us
    pallas_call x1, Pallas kernels, on_device(): pl.pallas_call(hand_out, out_shape=(block, block), in_specs=[inside] * 2,...  0.67 us

profile of v2, /device:TPU:20, one launch (start us, length us, event | category | flops | bytes accessed | tf_op | source)
XLA Modules:
  0.0 11.7 jit_solution(5533800316969568187)
XLA Ops:
  0.6 10.4 %shard_map.158 = (bf16[128,256]{1,0:T(8,128)(2,1)S(1)}, bf16[128,256]{1,0:T(8,128)(2,1)S(1)}) custom-call(bf16[128,256]{1,0:T(8,128)(2,1)} %refs_0_.1, f32[1,128]{1,0:T(1,128)} %bitcast.6, f32[1,256]{1,0:T(1,128)} %bitcast.4, bf16[256,768]{1,0:T(8,128)(2,1)} %refs_3_.1, bf16[128,256]{1,0:T(8,128)(2,1)} %refs_4_.1, bf16[256,256]{1,0:T(8,128)(2,1)} %refs_5_.1, ...), custom_call_target="tpu_custom_call" | custom-call | tf_op jit(solution)/shard_map/pallas_call | solution.py:276
  11.0 0.7 %shard_map.159 = (bf16[128,256]{1,0:T(8,128)(2,1)}, bf16[128,256]{1,0:T(8,128)(2,1)}) custom-call(bf16[128,256]{1,0:T(8,128)(2,1)S(1)} %get-tuple-element.4.a_ref, bf16[128,256]{1,0:T(8,128)(2,1)S(1)} %get-tuple-element.5.b_ref), custom_call_target="tpu_custom_call" | custom-call | tf_op jit(solution)/shard_map/pallas_call | solution.py:299

commit v3 on v2

--- a/solution.py
+++ b/solution.py
@@ -106,7 +106,7 @@
     hbm = refs[:15]
     pa_ref, pb_ref = refs[15:17]
     vm = refs[17:32]
-    (rim_ref, rim_rms_ref, filt_ref, signal_ref, carry_ref, state_ref, states_ref) = refs[32:39]
+    (product_ref, rim_ref, filt_ref, signal_ref, carry_ref, state_ref, states_ref) = refs[32:39]
     (load_sem, rim_send, rim_recv, st_send, st_recv, far_sem) = refs[39:]
     me = lax.axis_index("seq")
     rows, width = vm[0].shape
@@ -139,38 +139,34 @@
     (tok, rms_a, gain_a, proj_a, taps, out_a) = vm[:6]
     (rms_b, gain_b, proj_b, rates_ref, resid_ref, out_b, own_f, rim_f, back_f) = vm[6:]
 
-    crossing = jnp.logical_and(place == plane - 1, level < planes - 1)
-    pl.semaphore_wait(barrier, plane - 1 + level + crossing.astype(jnp.int32))
-
-    def rim_copies():
-        target = {"seq": lax.rem(me + 1, n)}
-        return [
-            pltpu.make_async_remote_copy(
-                src_ref=src,
-                dst_ref=dst,
-                send_sem=rim_send.at[i],
-                recv_sem=rim_recv.at[i],
-                device_id=target,
-                device_id_type=MESH,
-            )
-            for i, (src, dst) in enumerate(((hbm[0], rim_ref), (hbm[1], rim_rms_ref)))
-        ]
-
-    @pl.when(me < n - 1)
-    def _():
-        for copy in rim_copies():
-            copy.start()
-
-    @pl.loop(0, level)
-    def _(i):
-        signal(far_sem, i * plane + place)
-
     for i in (0, 1, 2, 3):
         loads[i].wait()
     normed = scaled(tok[...], column(rms_a[...]), gain_a[...])
     projected = dot(normed, proj_a[...])
     queries = projected[:, :width]
     product = (projected[:, width : 2 * width] * projected[:, 2 * width :]).astype(BF16)
+    product_ref[...] = product
+
+    crossing = jnp.logical_and(place == plane - 1, level < planes - 1)
+    pl.semaphore_wait(barrier, plane - 1 + level + crossing.astype(jnp.int32))
+
+    rim_copy = pltpu.make_async_remote_copy(
+        src_ref=product_ref,
+        dst_ref=rim_ref,
+        send_sem=rim_send,
+        recv_sem=rim_recv,
+        device_id={"seq": lax.rem(me + 1, n)},
+        device_id_type=MESH,
+    )
+
+    @pl.when(me < n - 1)
+    def _():
+        rim_copy.start()
+
+    @pl.loop(0, level)
+    def _(i):
+        signal(far_sem, i * plane + place)
+
     loads[12].wait()
     loads[4].wait()
     spectrum = dot(own_f[...], product)
@@ -199,12 +195,8 @@
 
     @pl.when(me > 0)
     def _():
-        for copy in rim_copies():
-            copy.wait_recv()
-        rim_normed = scaled(rim_ref[...], column(rim_rms_ref[...]), gain_a[...])
-        pair = dot(rim_normed, proj_a[:, width:])
-        rim_product = (pair[:, :width] * pair[:, width:]).astype(BF16)
-        carry_ref[...] = dot(rim_f[...], rim_product)
+        rim_copy.wait_recv()
+        carry_ref[...] = dot(rim_f[...], rim_ref[...])
 
     @pl.when(me == 0)
     def _():
@@ -254,8 +246,7 @@
 
     @pl.when(me < n - 1)
     def _():
-        for copy in rim_copies():
-            copy.wait_send()
+        rim_copy.wait_send()
 
     @pl.loop(0, n - 1 - me)
     def _(i):
@@ -281,15 +272,15 @@
             scratch_shapes=[pltpu.VMEM(a.shape, a.dtype) for a in args]
             + [
                 pltpu.VMEM((rows, width), BF16),
-                pltpu.VMEM((1, rows), F32),
+                pltpu.VMEM((rows, width), BF16),
                 pltpu.VMEM((rows, width), F32),
                 pltpu.VMEM((rows, width), F32),
                 pltpu.VMEM((2 * rows, width), F32),
                 pltpu.VMEM((modes, width), BF16),
                 pltpu.VMEM((n, modes, width), BF16),
                 pltpu.SemaphoreType.DMA((len(args),)),
-                pltpu.SemaphoreType.DMA((2,)),
-                pltpu.SemaphoreType.DMA((2,)),
+                pltpu.SemaphoreType.DMA,
+                pltpu.SemaphoreType.DMA,
                 pltpu.SemaphoreType.DMA((n,)),
                 pltpu.SemaphoreType.DMA((n,)),
                 pltpu.SemaphoreType.REGULAR,

time: 11.8 us -> 11.3 us (0.958)
  the two profiles are of different devices: /device:TPU:20 before, /device:TPU:12 now
where the time goes in v3:
time: 11.3 us; the launch traced here: 11.2 us
  Pallas kernels  10.6 us (94%)
  between operations  0.64 us (6%)
    pallas_call x1, Pallas kernels, on_device(): pl.pallas_call(functools.partial(kernel, n), out_shape=(fast, fast), in_s...  9.88 us
    pallas_call x1, Pallas kernels, on_device(): pl.pallas_call(hand_out, out_shape=(block, block), in_specs=[inside] * 2,...  0.67 us

profile of v3, /device:TPU:12, one launch (start us, length us, event | category | flops | bytes accessed | tf_op | source)
XLA Modules:
  0.0 11.2 jit_solution(10245839027864210373)
XLA Ops:
  0.6 9.9 %shard_map.158 = (bf16[128,256]{1,0:T(8,128)(2,1)S(1)}, bf16[128,256]{1,0:T(8,128)(2,1)S(1)}) custom-call(bf16[128,256]{1,0:T(8,128)(2,1)} %refs_0_.1, f32[1,128]{1,0:T(1,128)} %bitcast.6, f32[1,256]{1,0:T(1,128)} %bitcast.4, bf16[256,768]{1,0:T(8,128)(2,1)} %refs_3_.1, bf16[128,256]{1,0:T(8,128)(2,1)} %refs_4_.1, bf16[256,256]{1,0:T(8,128)(2,1)} %refs_5_.1, ...), custom_call_target="tpu_custom_call" | custom-call | tf_op jit(solution)/shard_map/pallas_call | solution.py:267
  10.5 0.7 %shard_map.159 = (bf16[128,256]{1,0:T(8,128)(2,1)}, bf16[128,256]{1,0:T(8,128)(2,1)}) custom-call(bf16[128,256]{1,0:T(8,128)(2,1)S(1)} %get-tuple-element.4.a_ref, bf16[128,256]{1,0:T(8,128)(2,1)S(1)} %get-tuple-element.5.b_ref), custom_call_target="tpu_custom_call" | custom-call | tf_op jit(solution)/shard_map/pallas_call | solution.py:290

commit v4 on v3

--- a/solution.py
+++ b/solution.py
@@ -223,13 +223,20 @@
             device_id_type=MESH,
         )
 
+    @pl.loop(me + 1, (level + 1) * plane)
+    def _(target):
+        state_copy(me, target).start()
+
     @pl.when(level < planes - 1)
     def _():
         pl.semaphore_wait(far_sem, planes - 1 - level)
 
-    @pl.loop(0, n - 1 - me)
-    def _(i):
-        state_copy(me, n - 1 - i).start()
+    @pl.loop(0, plane)
+    def _(i):
+        @pl.loop(0, planes - 1 - level)
+        def _(k):
+            state_copy(me, (planes - 1 - k) * plane + i).start()
+
 
     queries_b = dot(normed_b, proj_b[:, :width])
     local = dot(back_f[...], spectral_product(dot(own_f[...], signal), long_spec))

time: 11.3 us -> 11.1 us (0.982)
  the two profiles are of different devices: /device:TPU:12 before, /device:TPU:19 now
where the time goes in v4:
time: 11.1 us; the launch traced here: 11 us
  Pallas kernels  10.3 us (93%)
  between operations  0.64 us (6%)
    pallas_call x1, Pallas kernels, on_device(): pl.pallas_call(functools.partial(kernel, n), out_shape=(fast, fast), in_s...  9.66 us
    pallas_call x1, Pallas kernels, on_device(): pl.pallas_call(hand_out, out_shape=(block, block), in_specs=[inside] * 2,...  0.67 us

profile of v4, /device:TPU:19, one launch (start us, length us, event | category | flops | bytes accessed | tf_op | source)
XLA Modules:
  0.0 11.0 jit_solution(375361841407586796)
XLA Ops:
  0.6 9.7 %shard_map.158 = (bf16[128,256]{1,0:T(8,128)(2,1)S(1)}, bf16[128,256]{1,0:T(8,128)(2,1)S(1)}) custom-call(bf16[128,256]{1,0:T(8,128)(2,1)} %refs_0_.1, f32[1,128]{1,0:T(1,128)} %bitcast.6, f32[1,256]{1,0:T(1,128)} %bitcast.4, bf16[256,768]{1,0:T(8,128)(2,1)} %refs_3_.1, bf16[128,256]{1,0:T(8,128)(2,1)} %refs_4_.1, bf16[256,256]{1,0:T(8,128)(2,1)} %refs_5_.1, ...), custom_call_target="tpu_custom_call" | custom-call | tf_op jit(solution)/shard_map/pallas_call | solution.py:274
  10.3 0.7 %shard_map.159 = (bf16[128,256]{1,0:T(8,128)(2,1)}, bf16[128,256]{1,0:T(8,128)(2,1)}) custom-call(bf16[128,256]{1,0:T(8,128)(2,1)S(1)} %get-tuple-element.4.a_ref, bf16[128,256]{1,0:T(8,128)(2,1)S(1)} %get-tuple-element.5.b_ref), custom_call_target="tpu_custom_call" | custom-call | tf_op jit(solution)/shard_map/pallas_call | solution.py:297

commit v5 on v4

--- a/solution.py
+++ b/solution.py
@@ -139,6 +139,19 @@
     (tok, rms_a, gain_a, proj_a, taps, out_a) = vm[:6]
     (rms_b, gain_b, proj_b, rates_ref, resid_ref, out_b, own_f, rim_f, back_f) = vm[6:]
 
+    crossing = jnp.logical_and(place == plane - 1, level < planes - 1)
+
+    def meet(count):
+        pl.semaphore_wait(barrier, count)
+
+        @pl.loop(0, level)
+        def _(i):
+            signal(far_sem, i * plane + place)
+
+    @pl.when(jnp.logical_not(crossing))
+    def _():
+        meet(plane - 1 + level)
+
     for i in (0, 1, 2, 3):
         loads[i].wait()
     normed = scaled(tok[...], column(rms_a[...]), gain_a[...])
@@ -147,8 +160,9 @@
     product = (projected[:, width : 2 * width] * projected[:, 2 * width :]).astype(BF16)
     product_ref[...] = product
 
-    crossing = jnp.logical_and(place == plane - 1, level < planes - 1)
-    pl.semaphore_wait(barrier, plane - 1 + level + crossing.astype(jnp.int32))
+    @pl.when(crossing)
+    def _():
+        meet(plane + level)
 
     rim_copy = pltpu.make_async_remote_copy(
         src_ref=product_ref,
@@ -162,10 +176,6 @@
     @pl.when(me < n - 1)
     def _():
         rim_copy.start()
-
-    @pl.loop(0, level)
-    def _(i):
-        signal(far_sem, i * plane + place)
 
     loads[12].wait()
     loads[4].wait()

time: 11.1 us -> 11.2 us (level)
  the two profiles are of different devices: /device:TPU:19 before, /device:TPU:17 now
where the time goes in v5:
time: 11.2 us; the launch traced here: 11 us
  Pallas kernels  10.4 us (93%)
  between operations  0.64 us (6%)
    pallas_call x1, Pallas kernels, on_device(): pl.pallas_call(functools.partial(kernel, n), out_shape=(fast, fast), in_s...  9.7 us
    pallas_call x1, Pallas kernels, on_device(): pl.pallas_call(hand_out, out_shape=(block, block), in_specs=[inside] * 2,...  0.67 us

profile of v5, /device:TPU:17, one launch (start us, length us, event | category | flops | bytes accessed | tf_op | source)
XLA Modules:
  0.0 11.0 jit_solution(437747699457012951)
XLA Ops:
  0.6 9.7 %shard_map.158 = (bf16[128,256]{1,0:T(8,128)(2,1)S(1)}, bf16[128,256]{1,0:T(8,128)(2,1)S(1)}) custom-call(bf16[128,256]{1,0:T(8,128)(2,1)} %refs_0_.1, f32[1,128]{1,0:T(1,128)} %bitcast.6, f32[1,256]{1,0:T(1,128)} %bitcast.4, bf16[256,768]{1,0:T(8,128)(2,1)} %refs_3_.1, bf16[128,256]{1,0:T(8,128)(2,1)} %refs_4_.1, bf16[256,256]{1,0:T(8,128)(2,1)} %refs_5_.1, ...), custom_call_target="tpu_custom_call" | custom-call | tf_op jit(solution)/shard_map/pallas_call | solution.py:284
  10.3 0.7 %shard_map.159 = (bf16[128,256]{1,0:T(8,128)(2,1)}, bf16[128,256]{1,0:T(8,128)(2,1)}) custom-call(bf16[128,256]{1,0:T(8,128)(2,1)S(1)} %get-tuple-element.4.a_ref, bf16[128,256]{1,0:T(8,128)(2,1)S(1)} %get-tuple-element.5.b_ref), custom_call_target="tpu_custom_call" | custom-call | tf_op jit(solution)/shard_map/pallas_call | solution.py:307
